TPU v7x, 512 devices: a whole 4x4x16 slice. The times are simulated.
512 devices in a mesh: grp: 16 (over x, y), dev: 32 (over z, core).
Axes of the slice: x: 4, y: 4, z: 16, core: 2. Of those that a mesh axis runs over, the one named last changes fastest.
Arguments:
- coords: float32 [3, 65536], P(None, ('grp', 'dev')), may hold values from 0 to 1
- field: float32 [65536, 256], P(('grp', 'dev')), may hold values from -6 to 6
- observed: float32 [65536, 256], P(('grp', 'dev')), may hold values from -9 to 9
- pair_owner: int32 [16, 32], replicated, may hold values from 0 to 31, as said below
- cond_list: int32 [1024, 8], replicated, may hold values from 0 to 1023, as said below
- cond_mask: int32 [1024, 8], replicated, may hold values from 0 to 1, as said below
Outputs:
- field_out: float32 [65536, 256], P(('grp', 'dev'))
- last_grad: float32 [65536, 256], P(('grp', 'dev'))
Inputs may be any that keep to these rules, and one draw needn't show every extreme that they name: `pair_owner`: each row is a permutation of the device indices. `cond_list`: a used slot s < 6 of block b names an earlier block of b's group, a used slot s >= 6 a block of the group before; padded slots hold 0; for every group g and devices p, q of it, the used slots of the blocks stored on device p of group g and of those stored on device p of group g + 1 that name blocks stored on device q of group g name one block at most, and no more than one slot names it; this bound is reached. `cond_mask`: blocks of the first group and early blocks of a group have padded slots.
All inputs are finite; a program needn't handle non-finite values.
Results may differ from a plain program's by a relative error of at most 0.0017.
Values may be sent and summed in bfloat16 or wider, within the bound.
A program may use at most 64 MiB of HBM per device.

v0:
```python
import jax
import jax.numpy as jnp
from jax import lax
from jax.sharding import PartitionSpec as P

NCOND = 8
NSAME = 6
STEPS = 2
HIGH = lax.Precision.HIGHEST
LENGTH_SCALE = 0.35
NUGGET = 0.5
STEP_SIZE = 0.3


def shifted(block, axis, distance):
    devices = range(lax.axis_size(axis))
    route = [(i - distance, i) for i in devices if i - distance in devices]
    return lax.ppermute(block, axis, route)


def kernel_of(first, second):
    dist_sq = jnp.zeros((first.shape[1], second.shape[1]), jnp.float32)
    for coord in range(3):
        diff = first[coord][:, None] - second[coord][None, :]
        dist_sq = dist_sq + diff * diff
    return jnp.exp(-jnp.sqrt(dist_sq) / LENGTH_SCALE)


def factor_block(own_x, cond_x, point_mask):
    kcc = kernel_of(cond_x, cond_x) * point_mask[:, None] * point_mask[None, :]
    kcc = kcc + jnp.diag(NUGGET * point_mask + (1.0 - point_mask))
    kci = kernel_of(cond_x, own_x) * point_mask[:, None]
    count = own_x.shape[1]
    kii = kernel_of(own_x, own_x) + NUGGET * jnp.eye(count, dtype=jnp.float32)
    lower = jnp.linalg.cholesky(kcc)
    whiten = lax.linalg.triangular_solve(lower, kci, left_side=True, lower=True)
    regress = lax.linalg.triangular_solve(
        lower, whiten, left_side=True, lower=True, transpose_a=True
    )
    cond_cov = kii - jnp.dot(whiten.T, whiten, precision=HIGH)
    low_cov = jnp.linalg.cholesky(cond_cov)
    inv_low = lax.linalg.triangular_solve(
        low_cov, jnp.eye(count, dtype=jnp.float32), left_side=True, lower=True
    )
    precision = jnp.dot(inv_low.T, inv_low, precision=HIGH)
    return (regress, precision)


def body(coords, field, observed, pair_owner, cond_list, cond_mask):
    groups = lax.axis_size("grp")
    group_members = lax.axis_size("dev")
    my_group = lax.axis_index("grp")
    my_member = lax.axis_index("dev")
    points = field.shape[0] // 2
    out_cols = field.shape[1]
    cross_covariance = NCOND - NSAME
    member_ids = jnp.arange(group_members, dtype=jnp.int32)
    halves = jnp.arange(2, dtype=jnp.int32)
    inverse_factor = jnp.sum(
        jnp.where(
            pair_owner[:, :, None] == member_ids[None, None, :], member_ids[None, :, None], 0
        ),
        axis=1,
    )
    all_lists = cond_list.reshape(groups, group_members, 2, NCOND)
    all_masks = cond_mask.reshape(groups, group_members, 2, NCOND)
    next_group = jnp.minimum(my_group + 1, groups - 1)
    has_next = (my_group + 1 < groups).astype(jnp.int32)
    owner_here = pair_owner[my_group]
    base_id = my_group * 2 * group_members

    def locate(targets):
        pair_idx = jnp.clip((targets - base_id) // 2, 0, group_members - 1)
        return (owner_here[pair_idx], targets % 2)

    here_lists = all_lists[my_group][inverse_factor[my_group]]
    here_masks = all_masks[my_group][inverse_factor[my_group]]
    next_lists = all_lists[next_group][inverse_factor[next_group]][:, :, NSAME:]
    next_masks = all_masks[next_group][inverse_factor[next_group]][:, :, NSAME:] * has_next
    same_owner, same_half = locate(here_lists[:, :, :NSAME])
    fwd_owner, fwd_half = locate(next_lists)
    same_hit = (here_masks[:, :, :NSAME] * (same_owner == my_member))[..., None] * (
        same_half[..., None] == halves
    )
    fwd_hit = (next_masks * (fwd_owner == my_member))[..., None] * (fwd_half[..., None] == halves)
    selector = (jnp.sum(same_hit, axis=(1, 2)) + jnp.sum(fwd_hit, axis=(1, 2))).astype(jnp.float32)
    select_bf = selector.astype(jnp.bfloat16)
    same_valid = here_masks[my_member][:, :NSAME].reshape(-1).astype(jnp.float32)
    fwd_valid = next_masks[my_member].reshape(-1).astype(jnp.float32)
    req_owner = jnp.concatenate(
        [same_owner[my_member].reshape(-1), fwd_owner[my_member].reshape(-1)]
    )
    req_half = jnp.concatenate([same_half[my_member].reshape(-1), fwd_half[my_member].reshape(-1)])
    req_valid = jnp.concatenate([same_valid, fwd_valid])
    req_row = 2 * req_owner + req_half
    my_mask = here_masks[my_member].astype(jnp.float32)
    onehot_same = (
        (same_owner[my_member].reshape(-1)[:, None] == member_ids[None, :]) * same_valid[:, None]
    ).astype(jnp.bfloat16)
    onehot_fwd = (
        (fwd_owner[my_member].reshape(-1)[:, None] == member_ids[None, :]) * fwd_valid[:, None]
    ).astype(jnp.bfloat16)
    own_x = coords.reshape(3, 2, points).transpose(1, 0, 2)
    send_x = (
        selector[:, 0, None, None] * own_x[0][None] + selector[:, 1, None, None] * own_x[1][None]
    )
    recv_x = lax.all_to_all(send_x, "dev", split_axis=0, concat_axis=0, tiled=True)
    got_x = recv_x[req_owner]
    same_x = got_x[: 2 * NSAME].reshape(2, NSAME, 3, points)
    lift_x = shifted(got_x[2 * NSAME :].reshape(2, cross_covariance, 3, points), "grp", 1)
    cond_x = (
        jnp.concatenate([same_x, lift_x], axis=1)
        .transpose(0, 2, 1, 3)
        .reshape(2, 3, NCOND * points)
    )
    point_mask = jnp.repeat(my_mask, points, axis=1)
    regress, precision = jax.vmap(factor_block)(own_x, cond_x, point_mask)
    state = field.reshape(2, points, out_cols)
    target = observed.reshape(2, points, out_cols)
    slot_mask = my_mask[:, :, None, None]
    grad = jnp.zeros_like(state)
    for step_idx in range(STEPS):
        rounded = state.astype(jnp.bfloat16)
        piece = lax.all_gather(rounded, "dev", axis=0, tiled=True)
        rows = jnp.arange(piece.shape[0], dtype=jnp.int32)
        hit = ((req_row[:, None] == rows[None, :]) * req_valid[:, None]).astype(jnp.bfloat16)
        got = jnp.einsum("rn,npo->rpo", hit, piece, preferred_element_type=jnp.float32).astype(
            jnp.bfloat16
        )
        same = got[: 2 * NSAME].reshape(2, NSAME, points, out_cols)
        lifted = shifted(got[2 * NSAME :].reshape(2, cross_covariance, points, out_cols), "grp", 1)
        cond = jnp.concatenate([same, lifted], axis=1).astype(jnp.float32) * slot_mask
        cond = cond.reshape(2, NCOND * points, out_cols)
        resid = state - jnp.einsum("hnp,hno->hpo", regress, cond, precision=HIGH)
        scaled = jnp.einsum("hpq,hqo->hpo", precision, resid, precision=HIGH)
        back = jnp.einsum("hnp,hpo->hno", regress, scaled, precision=HIGH).reshape(
            2, NCOND, points, out_cols
        )
        back = (back * slot_mask).astype(jnp.bfloat16)
        dropped = shifted(back[:, NSAME:], "grp", -1)
        outgo = jnp.einsum(
            "rq,rpo->qpo",
            onehot_same,
            back[:, :NSAME].reshape(2 * NSAME, points, out_cols),
            preferred_element_type=jnp.float32,
        )
        outgo = outgo + jnp.einsum(
            "rq,rpo->qpo",
            onehot_fwd,
            dropped.reshape(2 * cross_covariance, points, out_cols),
            preferred_element_type=jnp.float32,
        )
        returned = lax.all_to_all(
            outgo.astype(jnp.bfloat16), "dev", split_axis=0, concat_axis=0, tiled=True
        )
        incoming = jnp.einsum(
            "qh,qpo->hpo", select_bf, returned, preferred_element_type=jnp.float32
        )
        grad = jnp.tanh(target - state) - (scaled - incoming)
        state = state + STEP_SIZE * grad
    return (state.reshape(2 * points, out_cols), grad.reshape(2 * points, out_cols))


def solution(mesh):
    placed = (
        P(None, ("grp", "dev")),
        P(("grp", "dev"), None),
        P(("grp", "dev"), None),
        P(),
        P(),
        P(),
    )
    return jax.shard_map(
        body,
        mesh=mesh,
        in_specs=placed,
        out_specs=(P(("grp", "dev"), None), P(("grp", "dev"), None)),
        check_vma=False,
    )
```

profile of v0, /device:TPU:3, one launch (start us, length us, event | category | flops | bytes accessed | tf_op | source)
XLA Modules:
  0.0 595.0 jit_solution(17836235499688568392)
XLA Ops:
  7.2 0.8 select_reduce_fusion
  8.0 1.0 copy.136
  9.0 1.0 copy.134
  9.9 0.7 fusion.113
  11.6 2.7 gather_fusion.1
  15.5 1.2 gather_fusion.4
  19.0 0.7 reshape.479
  19.7 15.9 %all-to-all-start = ((f32[32,1,192]{2,1,0:T(1,128)}), f32[32,1,192]{2,1,0:T(1,128)S(1)}, u32[]{:S(2)}, u32[]{:S(2)}) async-start(f32[32,1,192]{2,1,0:T(1,128)} %reshape.479), calls=%async_computation | async-start | bytes 65536 | tf_op jit(solution)/shard_map/all_to_all | solution.py:107
  35.7 0.6 convert_element_type.105
  39.4 0.7 pad_maximum_fusion.3
  40.1 7.6 %all-to-all-done = f32[32,1,192]{2,1,0:T(1,128)S(1)} async-done(((f32[32,1,192]{2,1,0:T(1,128)}), f32[32,1,192]{2,1,0:T(1,128)S(1)}, u32[]{:S(2)}, u32[]{:S(2)}) %all-to-all-start) | async-done | bytes 24608 | tf_op jit(solution)/shard_map/all_to_all | solution.py:107
  48.2 0.7 reduce.30
  49.6 3.2 collective-permute-start
  52.8 0.7 fusion.115
  53.5 2.6 collective-permute-done
  56.8 3.4 add_multiply_fusion
  60.3 1.3 copy-done
  61.6 23.6 %custom-call.43 = f32[2,128,128]{2,1,0:T(8,128)S(1)} custom-call(f32[2,128,128]{2,1,0:T(8,128)S(1)} %cholesky.314), custom_call_target="Cholesky" | custom-call | tf_op jit(solution)/shard_map/vmap(jit(cholesky))/cholesky | solution.py:35
  85.5 19.7 %custom-call.44 = f32[2,1,128,128]{2,3,1,0:T(8,128)S(1)} custom-call(f32[2,1,128,128]{3,2,1,0:T(8,128)S(1)} %select_bitcast_fusion.2), custom_call_target="InvertDiagBlocksLowerTriangular" | custom-call | tf_op jit(solution)/shard_map/vmap(jit(cholesky))/cholesky | solution.py:35
  105.2 1.5 constant_dynamic-update-slice_fusion.3
  106.7 1.5 convolution_subtract_fusion
  108.2 23.5 %custom-call.45 = f32[2,128,128]{2,1,0:T(8,128)S(1)} custom-call(f32[2,128,128]{2,1,0:T(8,128)S(1)} %cholesky.318), custom_call_target="Cholesky" | custom-call | tf_op jit(solution)/shard_map/vmap(jit(cholesky))/cholesky | solution.py:35
  131.7 19.9 %custom-call.46 = f32[2,1,128,128]{2,3,1,0:T(8,128)S(1)} custom-call(f32[2,1,128,128]{3,2,1,0:T(8,128)S(1)} %get-tuple-element.39), custom_call_target="InvertDiagBlocksLowerTriangular" | custom-call | tf_op jit(solution)/shard_map/vmap(jit(cholesky))/cholesky | solution.py:35
  152.0 1.6 convolution_subtract_fusion.1
  153.6 23.5 %custom-call.47 = f32[2,128,128]{2,1,0:T(8,128)S(1)} custom-call(f32[2,128,128]{2,1,0:T(8,128)S(1)} %cholesky.323), custom_call_target="Cholesky" | custom-call | tf_op jit(solution)/shard_map/vmap(jit(cholesky))/cholesky | solution.py:35
  177.0 19.7 %custom-call.48 = f32[2,1,128,128]{2,3,1,0:T(8,128)S(1)} custom-call(f32[2,1,128,128]{3,2,1,0:T(8,128)S(1)} %get-tuple-element.37), custom_call_target="InvertDiagBlocksLowerTriangular" | custom-call | tf_op jit(solution)/shard_map/vmap(jit(cholesky))/cholesky | solution.py:35
  197.0 1.5 convolution_subtract_fusion.2
  198.5 23.9 %custom-call.49 = f32[2,128,128]{2,1,0:T(8,128)S(1)} custom-call(f32[2,128,128]{2,1,0:T(8,128)S(1)} %convolution_subtract_fusion.2), custom_call_target="Cholesky" | custom-call | tf_op jit(solution)/shard_map/vmap(jit(cholesky))/cholesky | solution.py:35
  223.0 1.7 select_select_fusion
  224.7 14.2 %while.1 = (s32[]{:T(128)}, f32[2,512,512]{2,1,0:T(8,128)}, s32[4,2]{0,1:T(2,128)S(1)}, f32[4,2,128,128]{3,2,0,1:T(8,128)}, s32[]{:T(128)}) while((s32[]{:T(128)}, f32[2,512,512]{2,1,0:T(8,128)}, s32[4,2]{0,1:T(2,128)S(1)}, f32[4,2,128,128]{3,2,0,1:T(8,128)}, s32[]{:T(128)}) %tuple.51), condition=%wide.while_cond, body=%wide.while_body.sunk | while | flops 2 | bytes 263777 | solution.py:36
  225.4 2.9 bitcast_dynamic-update-slice_fusion.2
  228.9 2.9 bitcast_dynamic-update-slice_fusion.2
  232.5 2.9 bitcast_dynamic-update-slice_fusion.2
  236.1 2.9 bitcast_dynamic-update-slice_fusion.2
  239.0 79.4 %custom-call.50 = f32[2,4,128,128]{2,3,1,0:T(8,128)S(1)} custom-call(f32[2,4,128,128]{3,2,1,0:T(8,128)} %bitcast.203), custom_call_target="InvertDiagBlocksLowerTriangular" | custom-call | tf_op jit(solution)/shard_map/vmap()/triangular_solve | solution.py:36
  318.9 1.3 convolution_subtract_fusion.6
  320.5 1.4 convolution_subtract_fusion.8
  322.1 1.6 convolution_subtract_fusion.10
  324.7 11.7 %custom-call.51 = f32[2,64,64]{2,1,0:T(8,128)S(1)} custom-call(f32[2,64,64]{2,1,0:T(8,128)S(1)} %fusion.79), custom_call_target="Cholesky" | custom-call | tf_op jit(solution)/shard_map/vmap(jit(cholesky))/cholesky | solution.py:41
  336.7 10.0 %custom-call.52 = f32[2,1,64,64]{2,3,1,0:T(8,128)S(1)} custom-call(f32[2,1,64,64]{3,2,1,0:T(8,128)S(1)} %select_bitcast_fusion.3), custom_call_target="InvertDiagBlocksLowerTriangular" | custom-call | tf_op jit(solution)/shard_map/vmap()/triangular_solve | solution.py:42
  347.3 1.2 convolution_subtract_fusion.5
  348.8 1.3 convolution_subtract_fusion.7
  350.5 1.4 convolution_subtract_fusion.9
  352.3 2.8 fusion.4
  355.2 1.9 collective-permute-start.1
  357.6 5.5 collective-permute-done.1
  363.1 0.9 convolution_subtract_fusion.4
  364.3 1.0 fusion.134
  365.5 1.9 collective-permute-start.2
  368.0 3.2 collective-permute-done.2
  372.4 63.7 %all_to_all.15 = bf16[32,64,256]{2,1,0:T(8,128)(2,1)S(1)} all-to-all(bf16[32,64,256]{2,1,0:T(8,128)(2,1)S(1)} %copy.165), channel_id=1, replica_groups=mesh['grp'=16,'dev'=32] {'dev'}, dimensions={0} | all-to-all | bytes 2097152 | tf_op jit(solution)/shard_map/all_to_all | solution.py:153
  436.1 0.7 fusion.12
  436.8 0.7 fusion.136
  437.5 62.3 %all-gather.5.cloned.1.call-done = bf16[64,64,256]{2,1,0:T(8,128)(2,1)} async-done(((bf16[2,64,256]{2,1,0:T(8,128)(2,1)}), bf16[64,64,256]{2,1,0:T(8,128)(2,1)}) %all-gather.5.cloned.1.call-update) | async-done | bytes 2097168 | tf_op jit(solution)/shard_map/all_gather | solution.py:124
  499.8 2.8 fusion.7
  502.7 3.1 collective-permute-start.3
  506.0 5.5 collective-permute-done.3
  511.5 0.9 convolution_subtract_fusion.3
  512.7 1.0 fusion.133
  513.9 2.5 collective-permute-start.4
  516.9 2.7 collective-permute-done.4
  520.8 65.8 %all_to_all.16 = bf16[32,64,256]{2,1,0:T(8,128)(2,1)S(1)} all-to-all(bf16[32,64,256]{2,1,0:T(8,128)(2,1)S(1)} %copy.173), channel_id=1, replica_groups=mesh['grp'=16,'dev'=32] {'dev'}, dimensions={0} | all-to-all | bytes 2097152 | tf_op jit(solution)/shard_map/all_to_all | solution.py:153
  586.6 0.7 fusion.10
  587.2 0.7 multiply_add_fusion
  (193 shorter events, 22.1 us)
Async XLA Ops:
  15.5 3.2 copy-start.26
  15.5 20.1 %copy-start.1 = (f32[128,256]{1,0:T(8,128)S(1)}, f32[128,256]{1,0:T(8,128)}, u32[]{:S(2)}) copy-start(f32[128,256]{1,0:T(8,128)} %param.7) | copy-start | bytes 393220
  18.7 17.7 %copy-start.14 = (f32[32,2]{0,1:T(2,128)}, f32[32,2]{0,1:T(2,128)S(1)}, u32[]{:S(2)}) copy-start(f32[32,2]{0,1:T(2,128)S(1)} %add_convert_fusion.2) | copy-start | bytes 772
  19.7 28.0 %all-to-all-start = ((f32[32,1,192]{2,1,0:T(1,128)}), f32[32,1,192]{2,1,0:T(1,128)S(1)}, u32[]{:S(2)}, u32[]{:S(2)}) async-start(f32[32,1,192]{2,1,0:T(1,128)} %reshape.479), calls=%async_computation | async-start | bytes 65536 | tf_op jit(solution)/shard_map/all_to_all | solution.py:107
  35.6 316.7 %all-gather.3.cloned.1.call-start = ((), (), s32[]{:S(2)}) async-start(), calls=%async_computation.3 | async-start | bytes 2162688 | tf_op jit(solution)/shard_map/all_gather | solution.py:124
  36.3 463.4 %all-gather.5.cloned.1.call-start = ((), (), s32[]{:S(2)}) async-start(), calls=%async_computation.4 | async-start | bytes 2162688 | tf_op jit(solution)/shard_map/all_gather | solution.py:124
  36.5 2.5 copy-start.12
  38.0 18.2 %copy-start.18 = (s32[12]{0:T(128)}, s32[12]{0:T(128)S(1)}, u32[]{:S(2)}) copy-start(s32[12]{0:T(128)S(1)} %concatenate.79) | copy-start | bytes 148
  38.2 18.1 %copy-start.16 = (s32[4]{0:T(128)}, s32[4]{0:T(128)S(1)}, u32[]{:S(2)}) copy-start(s32[4]{0:T(128)S(1)} %concatenate.80) | copy-start | bytes 52
  39.3 10.3 %copy-start.21 = (bf16[4]{0:T(256)(128)(2,1)}, bf16[4]{0:T(256)(128)(2,1)S(1)}, u32[]{:S(2)}) copy-start(bf16[4]{0:T(256)(128)(2,1)S(1)} %convert_element_type.103) | copy-start | bytes 28
  39.4 10.2 %copy-start.23 = (bf16[12]{0:T(256)(128)(2,1)}, bf16[12]{0:T(256)(128)(2,1)S(1)}, u32[]{:S(2)}) copy-start(bf16[12]{0:T(256)(128)(2,1)S(1)} %convert_element_type.101) | copy-start | bytes 76
  49.6 6.5 %collective-permute-start = (f32[2,2,3,64]{3,1,0,2:T(2,128)S(1)}, f32[2,2,3,64]{3,1,0,2:T(2,128)S(1)}, u32[]{:S(2)}, u32[]{:S(2)}) collective-permute-start(f32[2,2,3,64]{3,1,0,2:T(2,128)S(1)} %copy.141), channel_id=1, source_target_pairs={{0,32},{32,64},{64,96},{96,128},{128,160},{160,192},{192,224},{224... | collective-permute-start | bytes 9224 | tf_op jit(solution)/shard_map/ppermute | solution.py:18
  56.2 0.6 copy-start.6
  56.2 0.6 copy-start.8
  56.2 0.6 copy-start.10
  60.2 1.3 copy-start
  222.9 1.8 copy-start.27
  223.0 95.4 %copy-start.4 = (f32[2,64]{1,0:T(2,128)S(1)}, f32[2,64]{1,0:T(2,128)}, u32[]{:S(2)}) copy-start(f32[2,64]{1,0:T(2,128)} %get-tuple-element.51) | copy-start | bytes 1540
  223.0 95.4 %copy-start.5 = (f32[2,64]{1,0:T(2,128)S(1)}, f32[2,64]{1,0:T(2,128)}, u32[]{:S(2)}) copy-start(f32[2,64]{1,0:T(2,128)} %get-tuple-element.52) | copy-start | bytes 1540
  223.0 95.4 %copy-start.7 = (f32[2,512]{1,0:T(2,128)S(1)}, f32[2,512]{1,0:T(2,128)}, u32[]{:S(2)}) copy-start(f32[2,512]{1,0:T(2,128)} %copy-done.6) | copy-start | bytes 12292
  223.0 95.4 %copy-start.9 = (f32[2,512]{1,0:T(2,128)S(1)}, f32[2,512]{1,0:T(2,128)}, u32[]{:S(2)}) copy-start(f32[2,512]{1,0:T(2,128)} %copy-done.8) | copy-start | bytes 12292
  223.0 95.4 %copy-start.11 = (f32[2,512]{1,0:T(2,128)S(1)}, f32[2,512]{1,0:T(2,128)}, u32[]{:S(2)}) copy-start(f32[2,512]{1,0:T(2,128)} %copy-done.10) | copy-start | bytes 12292
  239.0 97.5 %copy-start.3 = (pred[64,64]{1,0:T(8,128)(4,1)S(1)}, pred[64,64]{1,0:T(8,128)(4,1)}, u32[]{:S(2)}) copy-start(pred[64,64]{1,0:T(8,128)(4,1)} %iota_compare_fusion.7) | copy-start | bytes 12292
  323.8 28.5 %copy-start.20 = (s32[16]{0:T(128)S(1)}, s32[16]{0:T(128)}, u32[]{:S(2)}) copy-start(s32[16]{0:T(128)} %fusion.115) | copy-start | bytes 196
  323.8 28.5 %copy-start.25 = (bf16[16]{0:T(256)(128)(2,1)S(1)}, bf16[16]{0:T(256)(128)(2,1)}, u32[]{:S(2)}) copy-start(bf16[16]{0:T(256)(128)(2,1)} %pad_maximum_fusion.3) | copy-start | bytes 100
  355.2 7.8 %collective-permute-start.1 = (bf16[2,2,64,256]{3,2,1,0:T(8,128)(2,1)S(1)}, bf16[2,2,64,256]{3,2,1,0:T(8,128)(2,1)S(1)}, u32[]{:S(2)}, u32[]{:S(2)}) collective-permute-start(bf16[2,2,64,256]{3,2,1,0:T(8,128)(2,1)S(1)} %bitcast.195), channel_id=1, source_target_pairs={{0,32},{32,64},{64,96},{96,128},{128,160},{160,192},{192,224},{224... | collective-permute-start | bytes 393224 | tf_op jit(solution)/shard_map/ppermute | solution.py:18
  357.6 7.8 %copy-start.13 = (f32[2,8]{1,0:T(2,128)S(1)}, f32[2,8]{1,0:T(2,128)}, u32[]{:S(2)}) copy-start(f32[2,8]{1,0:T(2,128)} %copy-done.12) | copy-start | bytes 196
  364.3 3.2 copy-start.19
  364.3 3.2 copy-start.24
  365.5 5.8 copy-start.17
  365.5 5.8 copy-start.22
  365.5 5.7 collective-permute-start.2
  371.8 64.3 %copy-start.15 = (f32[32,2]{0,1:T(2,128)S(1)}, f32[32,2]{0,1:T(2,128)}, u32[]{:S(2)}) copy-start(f32[32,2]{0,1:T(2,128)} %copy-done.14) | copy-start | bytes 772
  372.4 64.3 %copy-start.2 = (f32[128,256]{1,0:T(8,128)S(1)}, f32[128,256]{1,0:T(8,128)}, u32[]{:S(2)}) copy-start(f32[128,256]{1,0:T(8,128)} %param.8) | copy-start | bytes 393220
  502.7 8.8 %collective-permute-start.3 = (bf16[2,2,64,256]{3,2,1,0:T(8,128)(2,1)S(1)}, bf16[2,2,64,256]{3,2,1,0:T(8,128)(2,1)S(1)}, u32[]{:S(2)}, u32[]{:S(2)}) collective-permute-start(bf16[2,2,64,256]{3,2,1,0:T(8,128)(2,1)S(1)} %bitcast.196), channel_id=1, source_target_pairs={{0,32},{32,64},{64,96},{96,128},{128,160},{160,192},{192,224},{224... | collective-permute-start | bytes 393224 | tf_op jit(solution)/shard_map/ppermute | solution.py:18
  513.9 5.7 collective-permute-start.4
Sparse Core Ops, SparseCore 0:
  39.1 73.2 all-gather.2
  437.6 62.1 all-gather.4
where the time goes:
time: 602 us; the launch traced here: 595 us
  other arithmetic  269 us (45%)
  blocking collectives  129 us (21%)
  waiting for transfers between devices  89.5 us (15%)
  local copies, waits for them, and re-layouts  31.7 us (5%)
  matrix products  31.7 us (5%)
  starting transfers between devices  28.6 us (5%)
  between operations  15.4 us (3%)
    another operation x18, other arithmetic, factor_block(): lower = jnp.linalg.cholesky(kcc)  154 us
    all_to_all x2, blocking collectives, body(): lax.all_to_all(outgo.astype(jnp.bfloat16), 'dev', split_axis=0, concat_ax...  129 us
    another operation x4, other arithmetic, factor_block(): whiten = lax.linalg.triangular_solve(lower, kci, left_side=True, lower=True)  81.8 us
    all_gather x2, waiting for transfers between devices, body(): piece = lax.all_gather(rounded, 'dev', axis=0, tiled=True)  62.4 us
    ppermute x5, waiting for transfers between devices, shifted(): return lax.ppermute(block, axis, route)  19.5 us
    all_to_all x1, starting transfers between devices, body(): lax.all_to_all(send_x, 'dev', split_axis=0, concat_axis=0, tiled=True)  15.9 us
    another operation x12, local copies, waits for them, and re-layouts  14.2 us
    ppermute x5, starting transfers between devices, shifted(): return lax.ppermute(block, axis, route)  12.6 us
  transfers between devices with their start and end apart: 8, of which 7 were waited for; matrix products, arithmetic and copies ran while one was open for 51% of the time, Pallas kernels for 0%

commit v1 on v0

--- a/solution.py
+++ b/solution.py
@@ -121,7 +121,10 @@
     grad = jnp.zeros_like(state)
     for step_idx in range(STEPS):
         rounded = state.astype(jnp.bfloat16)
-        piece = lax.all_gather(rounded, "dev", axis=0, tiled=True)
+        peers = lax.axis_size("dev")
+        blocks = jnp.stack([rounded for _ in range(peers)])
+        blocks = lax.all_to_all(blocks, "dev", split_axis=0, concat_axis=0)
+        piece = jnp.concatenate(blocks, axis=0)
         rows = jnp.arange(piece.shape[0], dtype=jnp.int32)
         hit = ((req_row[:, None] == rows[None, :]) * req_valid[:, None]).astype(jnp.bfloat16)
         got = jnp.einsum("rn,npo->rpo", hit, piece, preferred_element_type=jnp.float32).astype(

time: 602 us -> 654 us (1.086)
  blocking collectives: 129 us -> 237 us
  waiting for transfers between devices: 89.5 us -> 28.9 us
  local copies, waits for them, and re-layouts: 31.7 us -> 49.2 us
  between operations: 15.4 us -> 2.24 us
    all_to_all x0 -> x1, blocking collectives: none -> 104 us  [body(): blocks = lax.all_to_all(blocks, 'dev', split_axis=0, concat_axis=0)]
    all_gather x2 -> x0, waiting for transfers between devices: 62.4 us -> none  [body(): piece = lax.all_gather(rounded, 'dev', axis=0, tiled=True)]
    all_to_all x0 -> x2, local copies, waits for them, and re-layouts: none -> 7.55 us  [body(): blocks = lax.all_to_all(blocks, 'dev', split_axis=0, concat_axis=0)]
    another operation x12 -> x14, local copies, waits for them, and re-layouts: 14.2 us -> 19.6 us
  transfers between devices with their start and end apart: 8 -> 7, of which waited for: 7 -> 6; matrix products, arithmetic and copies ran while one was open for 51% -> 47% of each run, Pallas kernels for 0% -> 0%
where the time goes in v1:
time: 654 us; the launch traced here: 646 us
  other arithmetic  268 us (41%)
  blocking collectives  237 us (36%)
  local copies, waits for them, and re-layouts  49.2 us (8%)
  starting transfers between devices  32.3 us (5%)
  waiting for transfers between devices  28.9 us (4%)
  matrix products  28.6 us (4%)
    another operation x18, other arithmetic, factor_block(): lower = jnp.linalg.cholesky(kcc)  154 us
    all_to_all x2, blocking collectives, body(): lax.all_to_all(outgo.astype(jnp.bfloat16), 'dev', split_axis=0, concat_ax...  133 us
    all_to_all x1, blocking collectives, body(): blocks = lax.all_to_all(blocks, 'dev', split_axis=0, concat_axis=0)  104 us
    another operation x4, other arithmetic, factor_block(): whiten = lax.linalg.triangular_solve(lower, kci, left_side=True, lower=True)  81.8 us
    ppermute x5, waiting for transfers between devices, shifted(): return lax.ppermute(block, axis, route)  20.7 us
    all_to_all x1, starting transfers between devices, body(): lax.all_to_all(send_x, 'dev', split_axis=0, concat_axis=0, tiled=True)  15.9 us
    another operation x12, local copies, waits for them, and re-layouts  14.5 us
  transfers between devices with their start and end apart: 7, of which 6 were waited for; matrix products, arithmetic and copies ran while one was open for 47% of the time, Pallas kernels for 0%

profile of v1, /device:TPU:3, one launch (start us, length us, event | category | flops | bytes accessed | tf_op | source)
XLA Modules:
  0.0 645.7 jit_solution(3422968465358168883)
XLA Ops:
  0.6 0.8 select_reduce_fusion
  1.5 1.0 copy.140
  2.5 1.0 copy.138
  3.4 0.7 fusion.103
  5.1 2.7 gather_fusion.1
  9.0 1.2 gather_fusion.4
  12.4 0.7 reshape.492
  13.1 15.9 %all-to-all-start = ((f32[32,1,192]{2,1,0:T(1,128)}), f32[32,1,192]{2,1,0:T(1,128)S(1)}, u32[]{:S(2)}, u32[]{:S(2)}) async-start(f32[32,1,192]{2,1,0:T(1,128)} %reshape.492), calls=%async_computation | async-start | bytes 65536 | tf_op jit(solution)/shard_map/all_to_all | solution.py:107
  32.8 8.3 %all-to-all-done = f32[32,1,192]{2,1,0:T(1,128)S(1)} async-done(((f32[32,1,192]{2,1,0:T(1,128)}), f32[32,1,192]{2,1,0:T(1,128)S(1)}, u32[]{:S(2)}, u32[]{:S(2)}) %all-to-all-start) | async-done | bytes 24608 | tf_op jit(solution)/shard_map/all_to_all | solution.py:107
  41.1 3.2 stack.4
  44.4 5.5 all-to-all-start.1
  50.4 0.7 reduce.30
  51.8 3.2 collective-permute-start
  55.7 3.0 collective-permute-done
  58.8 3.4 add_multiply_fusion
  62.3 1.3 copy-done
  63.7 23.7 %custom-call.43 = f32[2,128,128]{2,1,0:T(8,128)S(1)} custom-call(f32[2,128,128]{2,1,0:T(8,128)S(1)} %cholesky.314), custom_call_target="Cholesky" | custom-call | tf_op jit(solution)/shard_map/vmap(jit(cholesky))/cholesky | solution.py:35
  87.6 19.7 %custom-call.44 = f32[2,1,128,128]{2,3,1,0:T(8,128)S(1)} custom-call(f32[2,1,128,128]{3,2,1,0:T(8,128)S(1)} %select_bitcast_fusion.2), custom_call_target="InvertDiagBlocksLowerTriangular" | custom-call | tf_op jit(solution)/shard_map/vmap(jit(cholesky))/cholesky | solution.py:35
  107.3 1.5 constant_dynamic-update-slice_fusion.3
  108.8 1.5 convolution_subtract_fusion
  110.3 23.5 %custom-call.45 = f32[2,128,128]{2,1,0:T(8,128)S(1)} custom-call(f32[2,128,128]{2,1,0:T(8,128)S(1)} %cholesky.318), custom_call_target="Cholesky" | custom-call | tf_op jit(solution)/shard_map/vmap(jit(cholesky))/cholesky | solution.py:35
  133.8 20.1 %custom-call.46 = f32[2,1,128,128]{2,3,1,0:T(8,128)S(1)} custom-call(f32[2,1,128,128]{3,2,1,0:T(8,128)S(1)} %get-tuple-element.39), custom_call_target="InvertDiagBlocksLowerTriangular" | custom-call | tf_op jit(solution)/shard_map/vmap(jit(cholesky))/cholesky | solution.py:35
  154.3 1.6 convolution_subtract_fusion.1
  155.9 23.5 %custom-call.47 = f32[2,128,128]{2,1,0:T(8,128)S(1)} custom-call(f32[2,128,128]{2,1,0:T(8,128)S(1)} %cholesky.323), custom_call_target="Cholesky" | custom-call | tf_op jit(solution)/shard_map/vmap(jit(cholesky))/cholesky | solution.py:35
  179.4 19.7 %custom-call.48 = f32[2,1,128,128]{2,3,1,0:T(8,128)S(1)} custom-call(f32[2,1,128,128]{3,2,1,0:T(8,128)S(1)} %get-tuple-element.37), custom_call_target="InvertDiagBlocksLowerTriangular" | custom-call | tf_op jit(solution)/shard_map/vmap(jit(cholesky))/cholesky | solution.py:35
  199.3 1.5 convolution_subtract_fusion.2
  200.8 23.6 %custom-call.49 = f32[2,128,128]{2,1,0:T(8,128)S(1)} custom-call(f32[2,128,128]{2,1,0:T(8,128)S(1)} %convolution_subtract_fusion.2), custom_call_target="Cholesky" | custom-call | tf_op jit(solution)/shard_map/vmap(jit(cholesky))/cholesky | solution.py:35
  225.1 1.8 select_select_fusion
  226.9 14.5 %while.1 = (s32[]{:T(128)}, f32[2,512,512]{2,1,0:T(8,128)}, s32[4,2]{0,1:T(2,128)S(1)}, f32[4,2,128,128]{3,2,0,1:T(8,128)}, s32[]{:T(128)}) while((s32[]{:T(128)}, f32[2,512,512]{2,1,0:T(8,128)}, s32[4,2]{0,1:T(2,128)S(1)}, f32[4,2,128,128]{3,2,0,1:T(8,128)}, s32[]{:T(128)}) %tuple.51), condition=%wide.while_cond, body=%wide.while_body.sunk | while | flops 2 | bytes 263777 | solution.py:36
  227.5 3.0 bitcast_dynamic-update-slice_fusion.2
  231.1 3.0 bitcast_dynamic-update-slice_fusion.2
  234.8 3.0 bitcast_dynamic-update-slice_fusion.2
  238.4 2.9 bitcast_dynamic-update-slice_fusion.2
  241.3 79.4 %custom-call.50 = f32[2,4,128,128]{2,3,1,0:T(8,128)S(1)} custom-call(f32[2,4,128,128]{3,2,1,0:T(8,128)} %bitcast.209), custom_call_target="InvertDiagBlocksLowerTriangular" | custom-call | tf_op jit(solution)/shard_map/vmap()/triangular_solve | solution.py:36
  321.3 1.3 convolution_subtract_fusion.6
  322.9 1.4 convolution_subtract_fusion.8
  324.5 1.6 convolution_subtract_fusion.10
  327.0 11.7 %custom-call.51 = f32[2,64,64]{2,1,0:T(8,128)S(1)} custom-call(f32[2,64,64]{2,1,0:T(8,128)S(1)} %fusion.69), custom_call_target="Cholesky" | custom-call | tf_op jit(solution)/shard_map/vmap(jit(cholesky))/cholesky | solution.py:41
  339.0 10.0 %custom-call.52 = f32[2,1,64,64]{2,3,1,0:T(8,128)S(1)} custom-call(f32[2,1,64,64]{3,2,1,0:T(8,128)S(1)} %select_bitcast_fusion.3), custom_call_target="InvertDiagBlocksLowerTriangular" | custom-call | tf_op jit(solution)/shard_map/vmap()/triangular_solve | solution.py:42
  349.7 1.2 convolution_subtract_fusion.5
  351.2 1.3 convolution_subtract_fusion.7
  352.9 1.4 convolution_subtract_fusion.9
  354.6 3.9 copy.165
  358.6 2.2 reshape.391
  360.8 2.0 convolution_convert_fusion.1
  363.0 1.9 collective-permute-start.1
  365.3 5.5 collective-permute-done.1
  370.8 0.9 convolution_subtract_fusion.4
  372.0 1.0 fusion.124
  373.3 1.9 collective-permute-start.2
  375.8 3.2 collective-permute-done.2
  380.2 70.9 %all_to_all.25 = bf16[32,64,256]{2,1,0:T(8,128)(2,1)S(1)} all-to-all(bf16[32,64,256]{2,1,0:T(8,128)(2,1)S(1)} %copy.170), channel_id=1, replica_groups=mesh['grp'=16,'dev'=32] {'dev'}, dimensions={0} | all-to-all | bytes 2097152 | tf_op jit(solution)/shard_map/all_to_all | solution.py:156
  451.9 1.9 stack.5
  453.8 104.2 %all_to_all.26 = bf16[32,2,64,256]{3,1,2,0:T(2,128)(2,1)S(1)} all-to-all(bf16[32,2,64,256]{3,1,2,0:T(2,128)(2,1)S(1)} %stack.5), channel_id=1, replica_groups=mesh['grp'=16,'dev'=32] {'dev'}, dimensions={0} | all-to-all | bytes 4194304 | tf_op jit(solution)/shard_map/all_to_all | solution.py:126
  558.0 3.7 copy.174
  561.6 2.7 reshape.397
  565.0 1.9 collective-permute-start.3
  567.0 5.8 collective-permute-done.3
  572.8 0.9 convolution_subtract_fusion.3
  574.0 1.0 fusion.123
  575.2 1.9 collective-permute-start.4
  577.7 3.2 collective-permute-done.4
  582.1 61.8 %all_to_all.27 = bf16[32,64,256]{2,1,0:T(8,128)(2,1)S(1)} all-to-all(bf16[32,64,256]{2,1,0:T(8,128)(2,1)S(1)} %copy.179), channel_id=1, replica_groups=mesh['grp'=16,'dev'=32] {'dev'}, dimensions={0} | all-to-all | bytes 2097152 | tf_op jit(solution)/shard_map/all_to_all | solution.py:156
  644.5 0.7 multiply_add_fusion
  (198 shorter events, 24.9 us)
Async XLA Ops:
  9.0 3.2 copy-start.26
  9.0 23.1 %copy-start.1 = (f32[128,256]{1,0:T(8,128)S(1)}, f32[128,256]{1,0:T(8,128)}, u32[]{:S(2)}) copy-start(f32[128,256]{1,0:T(8,128)} %param.7) | copy-start | bytes 393220
  12.2 17.2 %copy-start.14 = (f32[32,2]{0,1:T(2,128)}, f32[32,2]{0,1:T(2,128)S(1)}, u32[]{:S(2)}) copy-start(f32[32,2]{0,1:T(2,128)S(1)} %add_convert_fusion.2) | copy-start | bytes 772
  13.1 28.0 %all-to-all-start = ((f32[32,1,192]{2,1,0:T(1,128)}), f32[32,1,192]{2,1,0:T(1,128)S(1)}, u32[]{:S(2)}, u32[]{:S(2)}) async-start(f32[32,1,192]{2,1,0:T(1,128)} %reshape.492), calls=%async_computation | async-start | bytes 65536 | tf_op jit(solution)/shard_map/all_to_all | solution.py:107
  29.1 2.5 copy-start.12
  30.7 24.3 %copy-start.18 = (s32[12]{0:T(128)}, s32[12]{0:T(128)S(1)}, u32[]{:S(2)}) copy-start(s32[12]{0:T(128)S(1)} %concatenate.79) | copy-start | bytes 148
  30.8 24.2 %copy-start.16 = (s32[4]{0:T(128)}, s32[4]{0:T(128)S(1)}, u32[]{:S(2)}) copy-start(s32[4]{0:T(128)S(1)} %concatenate.80) | copy-start | bytes 52
  32.0 12.3 %copy-start.21 = (bf16[4]{0:T(256)(128)(2,1)}, bf16[4]{0:T(256)(128)(2,1)S(1)}, u32[]{:S(2)}) copy-start(bf16[4]{0:T(256)(128)(2,1)S(1)} %convert_element_type.105) | copy-start | bytes 28
  32.1 12.3 %copy-start.23 = (bf16[12]{0:T(256)(128)(2,1)}, bf16[12]{0:T(256)(128)(2,1)S(1)}, u32[]{:S(2)}) copy-start(bf16[12]{0:T(256)(128)(2,1)S(1)} %convert_element_type.103) | copy-start | bytes 76
  44.4 310.3 %all-to-all-start.1 = ((bf16[32,2,64,256]{3,1,2,0:T(2,128)(2,1)}), bf16[32,2,64,256]{3,1,2,0:T(2,128)(2,1)}, u32[]{:S(2)}, u32[]{:S(2)}) async-start(bf16[32,2,64,256]{3,1,2,0:T(2,128)(2,1)} %stack.4), calls=%async_computation.1 | async-start | bytes 4194304 | tf_op jit(solution)/shard_map/all_to_all | solution.py:126
  51.8 6.9 %collective-permute-start = (f32[2,2,3,64]{3,1,0,2:T(2,128)S(1)}, f32[2,2,3,64]{3,1,0,2:T(2,128)S(1)}, u32[]{:S(2)}, u32[]{:S(2)}) collective-permute-start(f32[2,2,3,64]{3,1,0,2:T(2,128)S(1)} %copy.145), channel_id=1, source_target_pairs={{0,32},{32,64},{64,96},{96,128},{128,160},{160,192},{192,224},{224... | collective-permute-start | bytes 9224 | tf_op jit(solution)/shard_map/ppermute | solution.py:18
  58.8 4.8 copy-start.6
  58.8 4.8 copy-start.8
  58.8 4.8 copy-start.10
  62.3 1.4 copy-start
  225.0 1.8 copy-start.27
  225.0 95.7 %copy-start.4 = (f32[2,64]{1,0:T(2,128)S(1)}, f32[2,64]{1,0:T(2,128)}, u32[]{:S(2)}) copy-start(f32[2,64]{1,0:T(2,128)} %get-tuple-element.51) | copy-start | bytes 1540
  225.0 95.7 %copy-start.5 = (f32[2,64]{1,0:T(2,128)S(1)}, f32[2,64]{1,0:T(2,128)}, u32[]{:S(2)}) copy-start(f32[2,64]{1,0:T(2,128)} %get-tuple-element.52) | copy-start | bytes 1540
  225.1 95.7 %copy-start.7 = (f32[2,512]{1,0:T(2,128)S(1)}, f32[2,512]{1,0:T(2,128)}, u32[]{:S(2)}) copy-start(f32[2,512]{1,0:T(2,128)} %copy-done.6) | copy-start | bytes 12292
  225.1 95.7 %copy-start.9 = (f32[2,512]{1,0:T(2,128)S(1)}, f32[2,512]{1,0:T(2,128)}, u32[]{:S(2)}) copy-start(f32[2,512]{1,0:T(2,128)} %copy-done.8) | copy-start | bytes 12292
  225.1 95.7 %copy-start.11 = (f32[2,512]{1,0:T(2,128)S(1)}, f32[2,512]{1,0:T(2,128)}, u32[]{:S(2)}) copy-start(f32[2,512]{1,0:T(2,128)} %copy-done.10) | copy-start | bytes 12292
  241.3 97.4 %copy-start.3 = (pred[64,64]{1,0:T(8,128)(4,1)S(1)}, pred[64,64]{1,0:T(8,128)(4,1)}, u32[]{:S(2)}) copy-start(pred[64,64]{1,0:T(8,128)(4,1)} %iota_compare_fusion.7) | copy-start | bytes 12292
  358.5 2.3 copy-start.20
  358.5 2.3 copy-start.25
  363.0 7.8 %collective-permute-start.1 = (bf16[2,2,64,256]{3,2,1,0:T(8,128)(2,1)S(1)}, bf16[2,2,64,256]{3,2,1,0:T(8,128)(2,1)S(1)}, u32[]{:S(2)}, u32[]{:S(2)}) collective-permute-start(bf16[2,2,64,256]{3,2,1,0:T(8,128)(2,1)S(1)} %bitcast.201), channel_id=1, source_target_pairs={{0,32},{32,64},{64,96},{96,128},{128,160},{160,192},{192,224},{224... | collective-permute-start | bytes 393224 | tf_op jit(solution)/shard_map/ppermute | solution.py:18
  365.3 7.7 %copy-start.13 = (f32[2,8]{1,0:T(2,128)S(1)}, f32[2,8]{1,0:T(2,128)}, u32[]{:S(2)}) copy-start(f32[2,8]{1,0:T(2,128)} %copy-done.12) | copy-start | bytes 196
  372.0 3.2 copy-start.19
  372.0 3.2 copy-start.24
  373.2 5.8 copy-start.17
  373.2 5.8 copy-start.22
  373.3 5.7 collective-permute-start.2
  379.6 71.5 %copy-start.15 = (f32[32,2]{0,1:T(2,128)S(1)}, f32[32,2]{0,1:T(2,128)}, u32[]{:S(2)}) copy-start(f32[32,2]{0,1:T(2,128)} %copy-done.14) | copy-start | bytes 772
  380.2 71.6 %copy-start.2 = (f32[128,256]{1,0:T(8,128)S(1)}, f32[128,256]{1,0:T(8,128)}, u32[]{:S(2)}) copy-start(f32[128,256]{1,0:T(8,128)} %param.8) | copy-start | bytes 393220
  565.0 7.8 %collective-permute-start.3 = (bf16[2,2,64,256]{3,2,1,0:T(8,128)(2,1)S(1)}, bf16[2,2,64,256]{3,2,1,0:T(8,128)(2,1)S(1)}, u32[]{:S(2)}, u32[]{:S(2)}) collective-permute-start(bf16[2,2,64,256]{3,2,1,0:T(8,128)(2,1)S(1)} %bitcast.202), channel_id=1, source_target_pairs={{0,32},{32,64},{64,96},{96,128},{128,160},{160,192},{192,224},{224... | collective-permute-start | bytes 393224 | tf_op jit(solution)/shard_map/ppermute | solution.py:18
  575.2 5.7 collective-permute-start.4
